TPU v7x, 32 devices: a whole 2x2x4 slice. The times are simulated.
32 devices in a mesh: group: 2 (over y), shard: 16 (over z, x, core).
Axes of the slice: x: 2, y: 2, z: 4, core: 2. Of those that a mesh axis runs over, the one named last changes fastest.
Arguments:
- samples: bfloat16 [32, 8192], P('shard'), may hold values from -6 to 6
- factor_old: float32 [8192, 8192], P('shard', 'group'), as said below
- damping: float32 [1], replicated, may hold values from 0.1 to 1
- gradients: bfloat16 [2048, 8192], P('shard', 'group'), may hold values from -6 to 6
Outputs:
- swept_factor: float32 [8192, 8192], P('shard', 'group')
- update: bfloat16 [8192, 2048], P('shard', 'group')
Inputs may be any that keep to these rules, and one draw needn't show every extreme that they name: factor_old is symmetric and positive definite.
All inputs are finite; a program needn't handle non-finite values.
Results may differ from a plain program's by a relative error of at most 0.0049.
Values may be sent and summed in bfloat16 or wider, within the bound.
A program may use at most 128 MiB of HBM per device.

v0:
```python
import jax
import jax.numpy as jnp
from jax import lax
from jax.sharding import PartitionSpec as P

D = 8192
BLOCK = 128
PIVOTS = 2
ema_keep = 0.5


def spread(block, axis, holder):
    block = jnp.where(lax.axis_index(axis) == holder, block, jnp.zeros_like(block))
    return lax.psum(block, axis)


def solve_spd(pivot_block, right_side):
    lower_factor = jnp.linalg.cholesky(pivot_block)
    half_solved = lax.linalg.triangular_solve(lower_factor, right_side, left_side=True, lower=True)
    return lax.linalg.triangular_solve(
        lower_factor, half_solved, left_side=True, lower=True, transpose_a=True
    )


def on_device(samples, factor_old, damping, gradients):
    row_count, col_count = factor_old.shape
    shard_index = lax.axis_index("shard")
    group_index = lax.axis_index("group")
    row_first = shard_index * row_count
    col_first = group_index * col_count
    total_tokens = samples.shape[0] * lax.axis_size("shard")
    contract = (((0,), (0,)), ((), ()))
    token_piece = lax.all_gather(samples, "shard", axis=0, tiled=True)
    left_part = lax.dynamic_slice_in_dim(token_piece, row_first, row_count, 1)
    right_part = lax.dynamic_slice_in_dim(token_piece, col_first, col_count, 1)
    covariance = lax.dot_general(
        left_part, right_part, contract, preferred_element_type=jnp.float32
    )
    row_ids = lax.broadcasted_iota(jnp.int32, (row_count, col_count), 0) + row_first
    col_ids = lax.broadcasted_iota(jnp.int32, (row_count, col_count), 1) + col_first
    diagonal = jnp.where(row_ids == col_ids, damping[0], 0.0)
    factor = ema_keep * factor_old + (1.0 - ema_keep) * (covariance / total_tokens) + diagonal
    spacing = D // PIVOTS
    sel_rows = lax.broadcasted_iota(jnp.int32, (BLOCK, col_count), 0)
    sel_cols = lax.broadcasted_iota(jnp.int32, (BLOCK, col_count), 1) + col_first

    def sweep_once(sweep_step, matrix):
        first_index = (sweep_step * spacing).astype(jnp.int32)
        col_owner = first_index // col_count
        row_owner = first_index // row_count
        col_offset = first_index - col_owner * col_count
        row_offset = first_index - row_owner * row_count
        own_columns = lax.dynamic_slice_in_dim(matrix, col_offset, BLOCK, 1)
        column = spread(own_columns, "group", col_owner)
        own_rows = lax.dynamic_slice_in_dim(matrix, row_offset, BLOCK, 0)
        own_pivot = lax.dynamic_slice_in_dim(column, row_offset, BLOCK, 0)
        pivot_strip, pivot_block = (
            spread(own_rows, "shard", row_owner),
            spread(own_pivot, "shard", row_owner),
        )
        selector = jnp.where(sel_cols == sel_rows + first_index, 1.0, 0.0).astype(jnp.float32)
        factor_q = solve_spd(pivot_block, pivot_strip + selector)
        matrix = matrix - jnp.dot(
            column, factor_q, precision=lax.Precision.HIGHEST, preferred_element_type=jnp.float32
        )
        addition = jnp.where(shard_index == row_owner, factor_q, 0.0)
        block_rows = lax.dynamic_slice_in_dim(matrix, row_offset, BLOCK, 0) + addition
        return lax.dynamic_update_slice_in_dim(matrix, block_rows, row_offset, 0)

    swept_factor = lax.fori_loop(0, PIVOTS, sweep_once, factor)
    swept_half = swept_factor.astype(jnp.bfloat16)
    partial_terms = lax.dot_general(
        swept_half,
        lax.all_gather(gradients, "shard", axis=0, tiled=True),
        (((1,), (1,)), ((), ())),
        preferred_element_type=jnp.float32,
    )
    update = lax.psum_scatter(partial_terms, "group", scatter_dimension=1, tiled=True).astype(
        jnp.bfloat16
    )
    return (swept_factor, update)


def solution(mesh):
    return jax.shard_map(
        on_device,
        mesh=mesh,
        in_specs=(P("shard", None), P("shard", "group"), P(), P("shard", "group")),
        out_specs=(P("shard", "group"), P("shard", "group")),
        check_vma=False,
    )
```

profile of v0, /device:TPU:0, one launch (start us, length us, event | category | flops | bytes accessed | tf_op | source)
XLA Modules:
  0.0 591.6 jit_solution(10280611587841758913)
XLA Ops:
  8.0 24.8 %all-gather = bf16[16,2,8192]{2,1,0:T(2,128)(2,1)S(1)} all-gather(bf16[1,2,8192]{2,1,0:T(2,128)(2,1)} %bitcast.32), channel_id=1, replica_groups=mesh['group'=2,'shard'=16] {'shard'}, dimensions={0}, use_global_device_ids=true | all-gather | bytes 557056 | tf_op jit(solution)/shard_map/all_gather | solution.py:33
  33.7 6.7 %select_add_fusion = f32[512,4096]{1,0:T(8,128)} fusion(f32[512,4096]{1,0:T(8,128)} %param.7, f32[]{:T(128)} %bitcast.31, s32[4096]{0:T(1024)S(1)} %iota_add_fusion.1, s32[512]{0:T(512)S(1)} %iota_add_fusion.2, bf16[32,8192]{1,0:T(8,128)(2,1)S(1)} %reshape.41, s32[]{:T(128)S(6)} %select_n.180, s32[]{:T(128)S(6)} %select_n.179), kind=kOutput, calls=%fused_computation.29 | convolution fusion | flops 146800640 | bytes 17090572 | tf_op jit(solution)/shard_map/dot_general | solution.py:36
  40.4 345.1 %while.17 = (s32[]{:T(128)}, f32[512,4096]{1,0:T(8,128)}, s32[]{:T(128)}, s32[4096]{0:T(1024)S(1)}, s32[]{:T(128)}, /*index=5*/s32[]{:T(128)}, s32[]{:T(128)}, s...) while((s32[]{:T(128)}, f32[512,4096]{1,0:T(8,128)}, ...), condition=%wide.region_6.7_spmd.clone, body=%wide.region_0.6_spmd.clone.sunk | while | flops 4838440960 | bytes 54937316 | solution.py:70
  40.4 1.7 dynamic-slice_select_fusion.6
  42.2 3.1 dynamic-slice_select_fusion.7
  45.3 19.4 %all-reduce.6.cloned.1.call-done = f32[512,128]{1,0:T(8,128)} async-done(((f32[512,128]{1,0:T(8,128)}), f32[512,128]{1,0:T(8,128)}) %all-reduce.6.cloned.1.call-update) | async-done | bytes 262160 | tf_op jit(solution)/shard_map/while/body/eval_jaxpr/psum | solution.py:14
  64.6 1.5 dynamic-slice_select_fusion.8
  66.1 101.6 %all-reduce.8.cloned.1.call-done = (f32[128,4096]{1,0:T(8,128)}, f32[128,128]{1,0:T(8,128)}) async-done(((f32[128,4096]{1,0:T(8,128)}, f32[128,128]{1,0:T(8,128)}), (f32[128,4096]{1,0:T(8,128)}, f32[128,128]{1,0:T(8,128)})) %all-reduce.8.cloned.1.call-update) | async-done | bytes 2162704 | tf_op jit(solution)/shard_map/while/body/eval_jaxpr/psum | solution.py:14
  167.7 0.9 copy.9
  168.6 0.9 fusion.45
  169.5 11.7 %cholesky.59 = f32[128,128]{1,0:T(8,128)S(1)} custom-call(f32[128,128]{1,0:T(8,128)S(1)} %fusion.45), custom_call_target="Cholesky" | custom-call | tf_op jit(solution)/shard_map/while/body/eval_jaxpr/jit(cholesky)/cholesky | solution.py:18
  182.6 9.8 %custom-call.26 = f32[1,128,128]{1,2,0:T(8,128)S(1)} custom-call(f32[1,128,128]{2,1,0:T(8,128)S(1)} %fusion.46), custom_call_target="InvertDiagBlocksLowerTriangular" | custom-call | tf_op jit(solution)/shard_map/while/body/eval_jaxpr/triangular_solve | solution.py:20
  192.4 3.6 fusion.47
  196.0 1.9 fusion.48
  197.9 11.1 %convolution_subtract_fusion.2 = f32[512,4096]{1,0:T(8,128)} fusion(f32[512,4096]{1,0:T(8,128)} %get-tuple-element.225, f32[512,128]{1,0:T(8,128)S(1)} %copy-done, f32[128,4096]{1,0:T(8,128)S(1)} %fusion.48), kind=kOutput, calls=%fused_computation.2.clone.1 | convolution fusion | flops 3223322624 | bytes 19136512 | tf_op jit(solution)/shard_map/while/body/eval_jaxpr/dot_general | solution.py:63
  209.1 3.2 add_dynamic-update-slice_fusion.2
  212.3 1.7 dynamic-slice_select_fusion.6
  214.1 3.1 dynamic-slice_select_fusion.7
  217.2 20.8 %all-reduce.6.cloned.1.call-done = f32[512,128]{1,0:T(8,128)} async-done(((f32[512,128]{1,0:T(8,128)}), f32[512,128]{1,0:T(8,128)}) %all-reduce.6.cloned.1.call-update) | async-done | bytes 262160 | tf_op jit(solution)/shard_map/while/body/eval_jaxpr/psum | solution.py:14
  237.9 1.5 dynamic-slice_select_fusion.8
  239.4 101.5 %all-reduce.8.cloned.1.call-done = (f32[128,4096]{1,0:T(8,128)}, f32[128,128]{1,0:T(8,128)}) async-done(((f32[128,4096]{1,0:T(8,128)}, f32[128,128]{1,0:T(8,128)}), (f32[128,4096]{1,0:T(8,128)}, f32[128,128]{1,0:T(8,128)})) %all-reduce.8.cloned.1.call-update) | async-done | bytes 2162704 | tf_op jit(solution)/shard_map/while/body/eval_jaxpr/psum | solution.py:14
  340.9 0.9 copy.9
  342.7 11.7 %cholesky.59 = f32[128,128]{1,0:T(8,128)S(1)} custom-call(f32[128,128]{1,0:T(8,128)S(1)} %fusion.45), custom_call_target="Cholesky" | custom-call | tf_op jit(solution)/shard_map/while/body/eval_jaxpr/jit(cholesky)/cholesky | solution.py:18
  355.7 9.8 %custom-call.26 = f32[1,128,128]{1,2,0:T(8,128)S(1)} custom-call(f32[1,128,128]{2,1,0:T(8,128)S(1)} %fusion.46), custom_call_target="InvertDiagBlocksLowerTriangular" | custom-call | tf_op jit(solution)/shard_map/while/body/eval_jaxpr/triangular_solve | solution.py:20
  365.6 3.6 fusion.47
  369.2 1.9 fusion.48
  371.1 11.1 %convolution_subtract_fusion.2 = f32[512,4096]{1,0:T(8,128)} fusion(f32[512,4096]{1,0:T(8,128)} %get-tuple-element.225, f32[512,128]{1,0:T(8,128)S(1)} %copy-done, f32[128,4096]{1,0:T(8,128)S(1)} %fusion.48), kind=kOutput, calls=%fused_computation.2.clone.1 | convolution fusion | flops 3223322624 | bytes 19136512 | tf_op jit(solution)/shard_map/while/body/eval_jaxpr/dot_general | solution.py:63
  382.2 3.2 add_dynamic-update-slice_fusion.2
  386.1 126.8 %all-gather.3.cloned.1.call-done = bf16[2048,4096]{1,0:T(8,128)(2,1)} async-done(((bf16[128,4096]{1,0:T(8,128)(2,1)}), bf16[2048,4096]{1,0:T(8,128)(2,1)}) %all-gather.3.cloned.1.call-update) | async-done | bytes 16777232 | tf_op jit(solution)/shard_map/all_gather | solution.py:74
  512.9 16.2 %fusion.20 = f32[512,2048]{1,0:T(8,128)} fusion(bf16[2048,4096]{1,0:T(8,128)(2,1)} %all-gather.3.cloned.1.call-done, f32[512,4096]{1,0:T(8,128)} %get-tuple-element.154), kind=kOutput, calls=%fused_computation.30 | convolution fusion | flops 8592031744 | bytes 29360128 | tf_op jit(solution)/shard_map/dot_general | solution.py:72
  529.1 52.6 %reduce-scatter.2.cloned.1.call-done = f32[512,1024]{1,0:T(8,128)} async-done(((f32[512,2048]{1,0:T(8,128)}), f32[512,1024]{1,0:T(8,128)}) %reduce-scatter.2.cloned.1.call-update) | async-done | bytes 2097168 | tf_op jit(solution)/shard_map/reduce_scatter | solution.py:78
  581.7 2.7 convert_element_type.7
  (26 shorter events, 4.5 us)
Async XLA Ops:
  40.4 24.2 %all-reduce.6.cloned.1.call-start = ((), (), s32[]{:S(2)}) async-start(), calls=%async_computation.3 | async-start | bytes 524288 | tf_op jit(solution)/shard_map/while/body/eval_jaxpr/psum | solution.py:14
  42.1 125.6 %all-reduce.8.cloned.1.call-start = ((), (), s32[]{:S(2)}) async-start(), calls=%async_computation.4 | async-start | bytes 4325376 | tf_op jit(solution)/shard_map/while/body/eval_jaxpr/psum | solution.py:14
  192.4 5.6 copy-start
  212.3 25.6 %all-reduce.6.cloned.1.call-start = ((), (), s32[]{:S(2)}) async-start(), calls=%async_computation.3 | async-start | bytes 524288 | tf_op jit(solution)/shard_map/while/body/eval_jaxpr/psum | solution.py:14
  214.0 126.9 %all-reduce.8.cloned.1.call-start = ((), (), s32[]{:S(2)}) async-start(), calls=%async_computation.4 | async-start | bytes 4325376 | tf_op jit(solution)/shard_map/while/body/eval_jaxpr/psum | solution.py:14
  365.6 5.6 copy-start
  385.5 127.5 %all-gather.3.cloned.1.call-start = ((), (), s32[]{:S(2)}) async-start(), calls=%async_computation.1 | async-start | bytes 17825792 | tf_op jit(solution)/shard_map/all_gather | solution.py:74
  386.0 195.7 %reduce-scatter.2.cloned.1.call-start = ((), (), s32[]{:S(2)}) async-start(), calls=%async_computation.2 | async-start | bytes 6291456 | tf_op jit(solution)/shard_map/reduce_scatter | solution.py:78
Sparse Core Ops, SparseCore 0:
  44.0 20.5 all-reduce.5
  68.8 98.8 all-reduce.7
  215.9 21.9 all-reduce.5
  241.9 98.9 all-reduce.7
Sparse Core Ops, SparseCore 1:
  388.1 124.8 all-gather.2
  529.2 52.5 reduce-scatter.1
where the time goes:
time: 592 us
  waiting for transfers between devices  423 us (71%)
  other arithmetic  69.1 us (12%)
  matrix products  56.1 us (9%)
  blocking collectives  24.8 us (4%)
  between operations  15.8 us (3%)
    psum x4, waiting for transfers between devices, spread(): return lax.psum(block, axis)  243 us
    all_gather x1, waiting for transfers between devices, on_device(): lax.all_gather(gradients, 'shard', axis=0, tiled=True)  127 us
    reduce_scatter x1, waiting for transfers between devices, on_device(): lax.psum_scatter(partial_terms, 'group', scatter_dimension=1, tiled=True)  52.6 us
    all_gather x1, blocking collectives, on_device(): token_piece = lax.all_gather(samples, 'shard', axis=0, tiled=True)  24.8 us
    another operation x6, other arithmetic, solve_spd(): lower_factor = jnp.linalg.cholesky(pivot_block)  24.8 us
    dot_general x2, matrix products, sweep_once(): jnp.dot(column, factor_q, precision=lax.Precision.HIGHEST, preferred_elem...  22.2 us
    another operation x4, other arithmetic, solve_spd(): lax.linalg.triangular_solve(lower_factor, half_solved, left_side=True, lo...  20.9 us
    dot_general x1, matrix products, on_device(): lax.dot_general(swept_half, lax.all_gather(gradients, 'shard', axis=0, ti...  16.2 us
  transfers between devices with their start and end apart: 6, of which 6 were waited for; matrix products, arithmetic and copies ran while one was open for 1% of the time, Pallas kernels for 0%

commit v1 on v0

--- a/solution.py
+++ b/solution.py
@@ -9,9 +9,15 @@
 ema_keep = 0.5
 
 
+def summed_here(x, axis):
+    terms = lax.all_gather(x, axis, axis=0, tiled=False)
+    total = terms.sum(axis=0)
+    return total
+
+
 def spread(block, axis, holder):
     block = jnp.where(lax.axis_index(axis) == holder, block, jnp.zeros_like(block))
-    return lax.psum(block, axis)
+    return summed_here(block, axis)
 
 
 def solve_spd(pivot_block, right_side):

time: 592 us -> 741 us (1.25)
  waiting for transfers between devices: 423 us -> 537 us
  other arithmetic: 69.1 us -> 90.5 us
  blocking collectives: 24.8 us -> 43.2 us
    all_gather x0 -> x4, waiting for transfers between devices: none -> 356 us  [summed_here(): terms = lax.all_gather(x, axis, axis=0, tiled=False)]
    psum x4 -> x0, waiting for transfers between devices: 243 us -> none  [spread(): return lax.psum(block, axis)]
    reduce_sum x0 -> x6, other arithmetic: none -> 26.1 us  [summed_here(): total = terms.sum(axis=0)]
    all_gather x0 -> x2, blocking collectives: none -> 18.4 us  [summed_here(): terms = lax.all_gather(x, axis, axis=0, tiled=False)]
  transfers between devices with their start and end apart: 6 -> 6, of which waited for: 6 -> 6; matrix products, arithmetic and copies ran while one was open for 1% -> 7% of each run, Pallas kernels for 0% -> 0%
where the time goes in v1:
time: 741 us; the launch traced here: 740 us
  waiting for transfers between devices  537 us (72%)
  other arithmetic  90.5 us (12%)
  matrix products  52.9 us (7%)
  blocking collectives  43.2 us (6%)
  between operations  15.8 us (2%)
    all_gather x4, waiting for transfers between devices, summed_here(): terms = lax.all_gather(x, axis, axis=0, tiled=False)  356 us
    all_gather x1, waiting for transfers between devices, on_device(): lax.all_gather(gradients, 'shard', axis=0, tiled=True)  128 us
    reduce_scatter x1, waiting for transfers between devices, on_device(): lax.psum_scatter(partial_terms, 'group', scatter_dimension=1, tiled=True)  52.6 us
    reduce_sum x6, other arithmetic, summed_here(): total = terms.sum(axis=0)  26.1 us
    all_gather x1, blocking collectives, on_device(): token_piece = lax.all_gather(samples, 'shard', axis=0, tiled=True)  24.8 us
    another operation x6, other arithmetic, solve_spd(): lower_factor = jnp.linalg.cholesky(pivot_block)  24.8 us
    dot_general x2, matrix products, sweep_once(): jnp.dot(column, factor_q, precision=lax.Precision.HIGHEST, preferred_elem...  22.2 us
    another operation x4, other arithmetic, solve_spd(): lax.linalg.triangular_solve(lower_factor, half_solved, left_side=True, lo...  20.9 us
  transfers between devices with their start and end apart: 6, of which 6 were waited for; matrix products, arithmetic and copies ran while one was open for 7% of the time, Pallas kernels for 0%

profile of v1, /device:TPU:0, one launch (start us, length us, event | category | flops | bytes accessed | tf_op | source)
XLA Modules:
  0.0 740.0 jit_solution(3140730088160505185)
XLA Ops:
  8.7 24.8 %all-gather.3 = bf16[16,2,8192]{2,1,0:T(2,128)(2,1)S(1)} all-gather(bf16[1,2,8192]{2,1,0:T(2,128)(2,1)} %bitcast.44), channel_id=1, replica_groups=mesh['group'=2,'shard'=16] {'shard'}, dimensions={0}, use_global_device_ids=true | all-gather | bytes 557056 | tf_op jit(solution)/shard_map/all_gather | solution.py:39
  33.7 6.7 select_add_fusion
  40.4 492.2 %while.17 = (s32[]{:T(128)}, f32[512,4096]{1,0:T(8,128)}, s32[]{:T(128)}, s32[4096]{0:T(1024)S(1)}, s32[]{:T(128)}, /*index=5*/s32[]{:T(128)}, s32[]{:T(128)}, s...) while((s32[]{:T(128)}, f32[512,4096]{1,0:T(8,128)}, ...), condition=%wide.region_6.7_spmd.clone, body=%wide.region_0.6_spmd.clone.sunk | while | flops 4846010368 | bytes 187975376 | solution.py:76
  40.4 1.0 dynamic-slice_select_fusion.6
  41.3 9.2 %all-gather.10 = f32[1024,128]{1,0:T(8,128)S(1)} all-gather(f32[512,128]{1,0:T(8,128)S(1)} %dynamic-slice_select_fusion.6), channel_id=2, replica_groups=mesh['group'=2,'shard'=16] {'group'}, dimensions={0}, use_global_device_ids=true | all-gather | bytes 786432 | tf_op jit(solution)/shard_map/while/body/eval_jaxpr/all_gather | solution.py:13
  51.3 3.1 dynamic-slice_select_fusion.7
  54.5 32.1 %all-gather.21.cloned.1.call-done = f32[2048,128]{1,0:T(8,128)} async-done(((f32[128,128]{1,0:T(8,128)}), f32[2048,128]{1,0:T(8,128)}) %all-gather.21.cloned.1.call-update) | async-done | bytes 1048592 | tf_op jit(solution)/shard_map/while/body/eval_jaxpr/all_gather | solution.py:13
  86.5 1.3 reduce_sum.59
  88.0 11.7 %cholesky.59 = f32[128,128]{1,0:T(8,128)S(1)} custom-call(f32[128,128]{1,0:T(8,128)S(1)} %fusion.45), custom_call_target="Cholesky" | custom-call | tf_op jit(solution)/shard_map/while/body/eval_jaxpr/jit(cholesky)/cholesky | solution.py:24
  101.0 9.8 %custom-call.26 = f32[1,128,128]{1,2,0:T(8,128)S(1)} custom-call(f32[1,128,128]{2,1,0:T(8,128)S(1)} %fusion.46), custom_call_target="InvertDiagBlocksLowerTriangular" | custom-call | tf_op jit(solution)/shard_map/while/body/eval_jaxpr/triangular_solve | solution.py:26
  110.8 144.5 %all-gather.19.cloned.1.call-done = f32[2048,4096]{1,0:T(8,128)} async-done(((f32[128,4096]{1,0:T(8,128)}), f32[2048,4096]{1,0:T(8,128)}) %all-gather.19.cloned.1.call-update) | async-done | bytes 33554448 | tf_op jit(solution)/shard_map/while/body/eval_jaxpr/all_gather | solution.py:13
  255.3 11.8 %reduce_sum.58 = f32[128,4096]{1,0:T(8,128)S(1)} reduce(f32[16,128,4096]{2,1,0:T(8,128)} %bitcast.41, f32[]{:T(128)} %constant.236.clone.12..sunk), dimensions={0}, to_apply=%region_5.5 | reduce | flops 7864320 | bytes 35651588 | tf_op jit(solution)/shard_map/while/body/eval_jaxpr/reduce_sum | solution.py:14
  267.0 2.0 fusion.47
  269.1 1.9 fusion.48
  271.0 11.1 %convolution_subtract_fusion.2 = f32[512,4096]{1,0:T(8,128)} fusion(f32[512,4096]{1,0:T(8,128)} %get-tuple-element.220, f32[512,128]{1,0:T(8,128)S(1)} %reduce_sum.57, f32[128,4096]{1,0:T(8,128)S(1)} %fusion.48), kind=kOutput, calls=%fused_computation.2.clone.1 | convolution fusion | flops 3223322624 | bytes 19136512 | tf_op jit(solution)/shard_map/while/body/eval_jaxpr/dot_general | solution.py:69
  282.1 3.2 add_dynamic-update-slice_fusion.2
  286.3 9.1 %all-gather.10 = f32[1024,128]{1,0:T(8,128)S(1)} all-gather(f32[512,128]{1,0:T(8,128)S(1)} %dynamic-slice_select_fusion.6), channel_id=2, replica_groups=mesh['group'=2,'shard'=16] {'group'}, dimensions={0}, use_global_device_ids=true | all-gather | bytes 786432 | tf_op jit(solution)/shard_map/while/body/eval_jaxpr/all_gather | solution.py:13
  296.2 3.1 dynamic-slice_select_fusion.7
  299.3 34.7 %all-gather.21.cloned.1.call-done = f32[2048,128]{1,0:T(8,128)} async-done(((f32[128,128]{1,0:T(8,128)}), f32[2048,128]{1,0:T(8,128)}) %all-gather.21.cloned.1.call-update) | async-done | bytes 1048592 | tf_op jit(solution)/shard_map/while/body/eval_jaxpr/all_gather | solution.py:13
  334.0 1.3 reduce_sum.59
  335.4 11.7 %cholesky.59 = f32[128,128]{1,0:T(8,128)S(1)} custom-call(f32[128,128]{1,0:T(8,128)S(1)} %fusion.45), custom_call_target="Cholesky" | custom-call | tf_op jit(solution)/shard_map/while/body/eval_jaxpr/jit(cholesky)/cholesky | solution.py:24
  348.5 9.8 %custom-call.26 = f32[1,128,128]{1,2,0:T(8,128)S(1)} custom-call(f32[1,128,128]{2,1,0:T(8,128)S(1)} %fusion.46), custom_call_target="InvertDiagBlocksLowerTriangular" | custom-call | tf_op jit(solution)/shard_map/while/body/eval_jaxpr/triangular_solve | solution.py:26
  358.3 144.3 %all-gather.19.cloned.1.call-done = f32[2048,4096]{1,0:T(8,128)} async-done(((f32[128,4096]{1,0:T(8,128)}), f32[2048,4096]{1,0:T(8,128)}) %all-gather.19.cloned.1.call-update) | async-done | bytes 33554448 | tf_op jit(solution)/shard_map/while/body/eval_jaxpr/all_gather | solution.py:13
  502.6 11.8 %reduce_sum.58 = f32[128,4096]{1,0:T(8,128)S(1)} reduce(f32[16,128,4096]{2,1,0:T(8,128)} %bitcast.41, f32[]{:T(128)} %constant.236.clone.12..sunk), dimensions={0}, to_apply=%region_5.5 | reduce | flops 7864320 | bytes 35651588 | tf_op jit(solution)/shard_map/while/body/eval_jaxpr/reduce_sum | solution.py:14
  514.3 2.0 fusion.47
  516.3 1.9 fusion.48
  518.2 11.1 %convolution_subtract_fusion.2 = f32[512,4096]{1,0:T(8,128)} fusion(f32[512,4096]{1,0:T(8,128)} %get-tuple-element.220, f32[512,128]{1,0:T(8,128)S(1)} %reduce_sum.57, f32[128,4096]{1,0:T(8,128)S(1)} %fusion.48), kind=kOutput, calls=%fused_computation.2.clone.1 | convolution fusion | flops 3223322624 | bytes 19136512 | tf_op jit(solution)/shard_map/while/body/eval_jaxpr/dot_general | solution.py:69
  529.4 3.2 add_dynamic-update-slice_fusion.2
  533.2 128.2 %all-gather.17.cloned.1.call-done = bf16[2048,4096]{1,0:T(8,128)(2,1)} async-done(((bf16[128,4096]{1,0:T(8,128)(2,1)}), bf16[2048,4096]{1,0:T(8,128)(2,1)}) %all-gather.17.cloned.1.call-update) | async-done | bytes 16777232 | tf_op jit(solution)/shard_map/all_gather | solution.py:80
  661.4 16.2 %fusion.20 = f32[512,2048]{1,0:T(8,128)} fusion(bf16[2048,4096]{1,0:T(8,128)(2,1)} %all-gather.17.cloned.1.call-done, f32[512,4096]{1,0:T(8,128)} %get-tuple-element.154), kind=kOutput, calls=%fused_computation.30 | convolution fusion | flops 8592031744 | bytes 29360128 | tf_op jit(solution)/shard_map/dot_general | solution.py:78
  677.6 52.6 %reduce-scatter.2.cloned.1.call-done = f32[512,1024]{1,0:T(8,128)} async-done(((f32[512,2048]{1,0:T(8,128)}), f32[512,1024]{1,0:T(8,128)}) %reduce-scatter.2.cloned.1.call-update) | async-done | bytes 2097168 | tf_op jit(solution)/shard_map/reduce_scatter | solution.py:84
  730.2 2.7 convert_element_type.7
  (30 shorter events, 6.2 us)
Async XLA Ops:
  40.4 46.2 %all-gather.21.cloned.1.call-start = ((), (), s32[]{:S(2)}) async-start(), calls=%async_computation.4 | async-start | bytes 1114112 | tf_op jit(solution)/shard_map/while/body/eval_jaxpr/all_gather | solution.py:13
  51.3 204.0 %all-gather.19.cloned.1.call-start = ((), (), s32[]{:S(2)}) async-start(), calls=%async_computation.3 | async-start | bytes 35651584 | tf_op jit(solution)/shard_map/while/body/eval_jaxpr/all_gather | solution.py:13
  285.3 48.7 %all-gather.21.cloned.1.call-start = ((), (), s32[]{:S(2)}) async-start(), calls=%async_computation.4 | async-start | bytes 1114112 | tf_op jit(solution)/shard_map/while/body/eval_jaxpr/all_gather | solution.py:13
  296.1 206.5 %all-gather.19.cloned.1.call-start = ((), (), s32[]{:S(2)}) async-start(), calls=%async_computation.3 | async-start | bytes 35651584 | tf_op jit(solution)/shard_map/while/body/eval_jaxpr/all_gather | solution.py:13
  532.6 128.8 %all-gather.17.cloned.1.call-start = ((), (), s32[]{:S(2)}) async-start(), calls=%async_computation.1 | async-start | bytes 17825792 | tf_op jit(solution)/shard_map/all_gather | solution.py:80
  533.1 197.0 %reduce-scatter.2.cloned.1.call-start = ((), (), s32[]{:S(2)}) async-start(), calls=%async_computation.2 | async-start | bytes 6291456 | tf_op jit(solution)/shard_map/reduce_scatter | solution.py:84
Sparse Core Ops, SparseCore 0:
  51.4 35.1 all-gather.20
  88.1 167.0 all-gather.18
  296.2 37.7 all-gather.20
  335.5 167.0 all-gather.18
Sparse Core Ops, SparseCore 1:
  535.2 126.1 all-gather.16
  677.6 52.5 reduce-scatter.1
